TPU v7x, 256 devices: a whole 4x4x8 slice. The times are simulated.
256 devices in a mesh: row: 16 (over y, x), col: 16 (over z, core).
Axes of the slice: x: 4, y: 4, z: 8, core: 2. Of those that a mesh axis runs over, the one named last changes fastest.
Arguments:
- rhs: float32 [128, 32768], P('row', 'col'), may hold values from -60 to 60
- flex_tiles: float32 [131072, 2048], P('row', 'col'), may hold values from -0.25 to 0.25
- flex_cols: int32 [256, 64], P('row', 'col'), may hold values from 0 to 15, as said below
- stiff_tiles: float32 [131072, 2048], P('row', 'col'), may hold values from -0.25 to 0.25
- stiff_cols: int32 [256, 64], P('row', 'col'), may hold values from 0 to 15, as said below
- deflation: float32 [512, 32768], P('row', 'col'), may hold values from -0.375 to 0.375
- coarse_rows: float32 [8192, 8192], P(('row', 'col')), may hold values from -5 to 5, as said below
- face_rows: int32 [64, 2048], P('row', 'col'), may hold values from 0 to 2047, as said below
- face_len: int32 [16, 64], P('row', 'col'), may hold values from 0 to 128, as said below
Outputs:
- solution: float32 [128, 32768], P('row', 'col')
- residual: float32 [128, 32768], P('row', 'col')
- correction: float32 [128, 32768], P('row', 'col')
Inputs may be any that keep to these rules, and one draw needn't show every extreme that they name: `flex_cols`: row b of a subdomain's block list names 4 different block columns, the first being b. `stiff_cols`: row b of a subdomain's block list names 4 different block columns, the first being b. `coarse_rows`: the whole matrix is symmetric. `face_rows`: the four lists of a subdomain name 512 different multipliers of it. `face_len`: the two subdomains of a face give it the same length; faces on the grid's boundary have length 0, inner faces at least 32.
All inputs are finite; a program needn't handle non-finite values.
Results may differ from a plain program's by a relative error of at most 0.0003.
Values sent between devices are 32-bit elements; how exact they have to be, the bound alone decides.
A program may use at most 64 MiB of HBM per device.

v0:
```python
import jax
import jax.numpy as jnp
from jax import lax
from jax.sharding import PartitionSpec as P

ITERS = 3
PRECISE = lax.Precision.HIGHEST


def with_halo(cells, sides, width):
    for axis, dim in sides:
        count = lax.axis_size(axis)
        ends = count - 1
        head = lax.slice_in_dim(cells, 0, width, axis=dim)
        tail = lax.slice_in_dim(cells, cells.shape[dim] - width, cells.shape[dim], axis=dim)
        cells = jnp.concatenate(
            [
                lax.ppermute(tail, axis, [(i, (i + 1) % count) for i in range(ends)]),
                cells,
                lax.ppermute(head, axis, [((i + 1) % count, i) for i in range(ends)]),
            ],
            axis=dim,
        )
    return cells


def sparse_forward(vector, tile_set, columns):
    load_count = vector.shape[0]
    blocks, per_row = columns.shape
    tile_width = tile_set.shape[-1]
    pieces = vector.reshape(load_count, blocks, tile_width)
    picked = jnp.take(pieces, columns.reshape(-1), axis=1).reshape(
        load_count, blocks, per_row, tile_width
    )
    product = jnp.einsum("lbkw,bkwv->lbv", picked, tile_set, precision=PRECISE)
    return product.reshape(load_count, blocks * tile_width)


def sparse_backward(vector, tile_set, columns):
    load_count = vector.shape[0]
    blocks, per_row = columns.shape
    tile_width = tile_set.shape[-1]
    pieces = vector.reshape(load_count, blocks, tile_width)
    product = jnp.einsum("lbv,bkwv->lbkw", pieces, tile_set, precision=PRECISE)
    onehot = (columns[:, :, None] == jnp.arange(blocks, dtype=jnp.int32)[None, None, :]).astype(
        jnp.float32
    )
    summed = jnp.einsum("lbkw,bkj->ljw", product, onehot, precision=PRECISE)
    return summed.reshape(load_count, blocks * tile_width)


def pair_totals(first_field, second_field, third_field, fourth_field):
    return lax.psum(
        (jnp.sum(first_field * second_field, axis=1), jnp.sum(third_field * fourth_field, axis=1)),
        ("row", "col"),
    )


def shards(
    rhs, flex_tiles, flex_cols, stiff_tiles, stiff_cols, deflation, coarse_rows, face_rows, face_len
):
    blocks, per_row = flex_cols.shape
    tile_width = flex_tiles.shape[1]
    flex_set = flex_tiles.reshape(blocks, per_row, tile_width, tile_width)
    stiff_set = stiff_tiles.reshape(blocks, per_row, tile_width, tile_width)
    face_width = face_rows.shape[1]
    flat_index = face_rows.reshape(-1)
    slots = jnp.arange(face_width, dtype=jnp.int32)
    live_mask = (slots[None, :] < face_len.reshape(4, 1)).astype(jnp.float32)

    def face_part(vector):
        load_count = vector.shape[0]
        traces = jnp.take(vector, flat_index, axis=1).reshape(load_count, 4, face_width)
        across_rows = with_halo(traces[:, 0:2], (("row", 1),), 1)
        across_cols = with_halo(traces[:, 2:4], (("col", 1),), 1)
        partner = jnp.stack(
            [across_rows[:, 0], across_rows[:, 3], across_cols[:, 0], across_cols[:, 3]], axis=1
        )
        jump_values = (traces - partner) * live_mask[None]
        return (
            jnp.zeros_like(vector)
            .at[:, flat_index]
            .add(jump_values.reshape(load_count, 4 * face_width))
        )

    def operate(vector):
        coupling = face_part(vector)
        after_flex = sparse_forward(vector, flex_set, flex_cols)
        after_stiff = sparse_forward(after_flex, stiff_set, stiff_cols)
        back_stiff = sparse_backward(after_stiff, stiff_set, stiff_cols)
        local_part = sparse_backward(back_stiff, flex_set, flex_cols)
        return vector + local_part + coupling

    def precondition(vector):
        coefficients = jnp.einsum("lm,dm->ld", vector, deflation, precision=PRECISE)
        energy = jnp.einsum(
            "ln,dn->ld",
            lax.all_gather(coefficients, ("row", "col"), axis=1, tiled=True),
            coarse_rows,
            precision=PRECISE,
        )
        return vector + jnp.einsum("ld,dm->lm", energy, deflation, precision=PRECISE)

    residual = rhs
    solution = jnp.zeros_like(rhs)
    correction = precondition(residual)
    direction = correction
    image = operate(direction)
    curvature_sum, descent_sum = pair_totals(direction, image, residual, direction)
    for iteration in range(ITERS):
        step_size = (descent_sum / curvature_sum)[:, None]
        solution = solution + step_size * direction
        residual = residual - step_size * image
        correction = precondition(residual)
        if iteration + 1 < ITERS:
            cross_sum = lax.psum(jnp.sum(correction * image, axis=1), ("row", "col"))
            blend = -cross_sum / curvature_sum
            direction = correction + blend[:, None] * direction
            image = operate(direction)
            curvature_sum, descent_sum = pair_totals(direction, image, residual, direction)
    return (solution, residual, correction)


def solution(mesh):
    return jax.shard_map(
        shards,
        mesh=mesh,
        in_specs=(
            P("row", "col"),
            P("row", "col"),
            P("row", "col"),
            P("row", "col"),
            P("row", "col"),
            P("row", "col"),
            P(("row", "col"), None),
            P("row", "col"),
            P("row", "col"),
        ),
        out_specs=(P("row", "col"), P("row", "col"), P("row", "col")),
        check_vma=False,
    )
```

profile of v0, /device:TPU:1, one launch (start us, length us, event | category | flops | bytes accessed | tf_op | source)
XLA Modules:
  0.0 747.8 jit_solution(5366016694959184341)
XLA Ops:
  0.7 0.8 compare_select_fusion.1
  1.5 0.7 compare_and_fusion
  2.1 1.2 convolution_bitcast_fusion.21
  3.4 67.8 %all-gather = f32[256,32,8]{1,2,0:T(8,128)S(1)} all-gather(f32[1,32,8]{1,2,0:T(8,128)S(1)} %convolution_bitcast_fusion.21), channel_id=1, replica_groups=mesh['row'=16,'col'=16] {'row','col'}, dimensions={0}, use_global_device_ids=true | all-gather | bytes 263168 | tf_op jit(solution)/shard_map/all_gather | solution.py:98
  71.9 0.9 fusion.36
  73.5 1.0 gather_fusion.2
  74.7 2.6 collective-permute-start
  77.4 1.3 collective-permute-start.1
  78.8 1.9 collective-permute-start.2
  80.8 2.7 collective-permute-start.3
  84.8 3.8 convolution_bitcast_fusion.17
  89.4 4.0 convolution_bitcast_fusion.16
  93.5 3.6 convolution_bitcast_fusion.5
  97.4 3.6 convolution_bitcast_fusion.4
  102.2 4.2 scatter_custom_fusion
  106.9 78.0 %all-reduce.2 = (f32[8]{0:T(128)S(1)}, f32[8]{0:T(128)S(1)}) all-reduce(f32[8]{0:T(128)S(1)} %get-tuple-element.10, f32[8]{0:T(128)S(1)} %get-tuple-element.9), channel_id=1, replica_groups=mesh['row'=16,'col'=16] {'row','col'}, use_global_device_ids=true, to_apply=%region_1.2 | all-reduce | flops 16 | bytes 128 | tf_op jit(solution)/shard_map/psum | solution.py:53
  185.2 60.6 %all-gather.1 = f32[256,32,8]{1,2,0:T(8,128)S(1)} all-gather(f32[1,32,8]{1,2,0:T(8,128)S(1)} %convolution_bitcast_fusion.20), channel_id=1, replica_groups=mesh['row'=16,'col'=16] {'row','col'}, dimensions={0}, use_global_device_ids=true | all-gather | bytes 263168 | tf_op jit(solution)/shard_map/all_gather | solution.py:98
  246.5 0.9 fusion.37
  247.8 75.0 %psum.58 = f32[8]{0:T(128)S(1)} all-reduce(f32[8]{0:T(128)S(1)} %get-tuple-element.31), channel_id=1, replica_groups=mesh['row'=16,'col'=16] {'row','col'}, use_global_device_ids=true, to_apply=%region_6.9 | all-reduce | flops 8 | bytes 64 | tf_op jit(solution)/shard_map/psum | solution.py:116
  323.3 1.0 gather_fusion.5
  324.6 1.6 collective-permute-start.4
  326.2 1.3 collective-permute-start.5
  327.5 4.5 collective-permute-start.6
  332.1 2.1 collective-permute-start.7
  335.0 3.8 convolution_bitcast_fusion.15
  339.7 4.0 convolution_bitcast_fusion.14
  343.7 3.6 convolution_bitcast_fusion.3
  347.6 3.6 convolution_bitcast_fusion.2
  352.4 3.9 scatter_custom_fusion.1
  356.8 77.0 %all-reduce.1 = (f32[8]{0:T(128)S(1)}, f32[8]{0:T(128)S(1)}) all-reduce(f32[8]{0:T(128)S(1)} %get-tuple-element.8, f32[8]{0:T(128)S(1)} %get-tuple-element.7), channel_id=1, replica_groups=mesh['row'=16,'col'=16] {'row','col'}, use_global_device_ids=true, to_apply=%region_8.11 | all-reduce | flops 16 | bytes 128 | tf_op jit(solution)/shard_map/psum | solution.py:53
  434.1 61.9 %all-gather.2 = f32[256,32,8]{1,2,0:T(8,128)S(1)} all-gather(f32[1,32,8]{1,2,0:T(8,128)S(1)} %convolution_bitcast_fusion.19), channel_id=1, replica_groups=mesh['row'=16,'col'=16] {'row','col'}, dimensions={0}, use_global_device_ids=true | all-gather | bytes 263168 | tf_op jit(solution)/shard_map/all_gather | solution.py:98
  496.7 0.9 fusion.38
  498.0 73.7 %psum.61 = f32[8]{0:T(128)S(1)} all-reduce(f32[8]{0:T(128)S(1)} %get-tuple-element.33), channel_id=1, replica_groups=mesh['row'=16,'col'=16] {'row','col'}, use_global_device_ids=true, to_apply=%region_13.16 | all-reduce | flops 8 | bytes 64 | tf_op jit(solution)/shard_map/psum | solution.py:116
  572.1 1.0 gather_fusion.8
  573.4 3.8 collective-permute-start.10
  577.3 1.9 collective-permute-start.11
  579.2 2.0 collective-permute-start.8
  581.3 1.7 collective-permute-start.9
  583.8 3.8 convolution_bitcast_fusion.13
  588.4 4.0 convolution_bitcast_fusion.12
  592.4 3.6 convolution_bitcast_fusion.1
  596.4 3.6 convolution_bitcast_fusion
  601.1 3.9 scatter_custom_fusion.2
  605.5 77.2 %all-reduce = (f32[8]{0:T(128)S(1)}, f32[8]{0:T(128)S(1)}) all-reduce(f32[8]{0:T(128)S(1)} %get-tuple-element.6, f32[8]{0:T(128)S(1)} %get-tuple-element.5), channel_id=1, replica_groups=mesh['row'=16,'col'=16] {'row','col'}, use_global_device_ids=true, to_apply=%region_15.18 | all-reduce | flops 16 | bytes 128 | tf_op jit(solution)/shard_map/psum | solution.py:53
  682.7 0.7 multiply_subtract_fusion
  683.7 61.3 %all-gather.3 = f32[256,32,8]{1,2,0:T(8,128)S(1)} all-gather(f32[1,32,8]{1,2,0:T(8,128)S(1)} %convolution_bitcast_fusion.18), channel_id=1, replica_groups=mesh['row'=16,'col'=16] {'row','col'}, dimensions={0}, use_global_device_ids=true | all-gather | bytes 263168 | tf_op jit(solution)/shard_map/all_gather | solution.py:98
  745.8 0.9 fusion.39
  746.7 0.9 convolution_add_fusion
  (137 shorter events, 18.0 us)
Async XLA Ops:
  0.6 71.3 %copy-start = (f32[32,8192]{1,0:T(8,128)S(1)}, f32[32,8192]{1,0:T(8,128)}, u32[]{:S(2)}) copy-start(f32[32,8192]{1,0:T(8,128)} %param.19) | copy-start | bytes 3145732
  0.6 72.2 %copy-start.8 = (f32[8,2048]{1,0:T(8,128)S(1)}, f32[8,2048]{1,0:T(8,128)}, u32[]{:S(2)}) copy-start(f32[8,2048]{1,0:T(8,128)} %param.13) | copy-start | bytes 196612
  0.7 72.2 %copy-start.7 = (f32[32,2048]{1,0:T(8,128)S(1)}, f32[32,2048]{1,0:T(8,128)}, u32[]{:S(2)}) copy-start(f32[32,2048]{1,0:T(8,128)} %param.18) | copy-start | bytes 786436
  3.4 80.1 %copy-start.11 = (s32[16,4]{0,1:T(4,128)S(1)}, s32[16,4]{0,1:T(4,128)}, u32[]{:S(2)}) copy-start(s32[16,4]{0,1:T(4,128)} %param.15) | copy-start | bytes 772
  3.4 80.3 %copy-start.10 = (s32[16,4]{0,1:T(4,128)S(1)}, s32[16,4]{0,1:T(4,128)}, u32[]{:S(2)}) copy-start(s32[16,4]{0,1:T(4,128)} %param.17) | copy-start | bytes 772
  3.4 80.5 %copy-start.13 = (s32[1,4]{1,0:T(1,128)S(1)}, s32[1,4]{1,0:T(1,128)}, u32[]{:S(2)}) copy-start(s32[1,4]{1,0:T(1,128)} %param.21) | copy-start | bytes 52
  74.7 27.1 %collective-permute-start = (f32[8,1,128]{2,0,1:T(8,128)S(1)}, f32[8,1,128]{2,0,1:T(8,128)S(1)}, u32[]{:S(2)}, u32[]{:S(2)}) collective-permute-start(f32[8,1,128]{2,0,1:T(8,128)S(1)} %copy.118), channel_id=1, source_target_pairs={{0,16},{16,32},{32,48},{48,64},{64,80},{80,96},{96,112},{112,128},... | collective-permute-start | bytes 12296 | tf_op jit(solution)/shard_map/ppermute | solution.py:18
  77.4 24.4 %collective-permute-start.1 = (f32[8,1,128]{2,0,1:T(8,128)S(1)}, f32[8,1,128]{2,0,1:T(8,128)S(1)}, u32[]{:S(2)}, u32[]{:S(2)}) collective-permute-start(f32[8,1,128]{2,0,1:T(8,128)S(1)} %copy.119), channel_id=1, source_target_pairs={{16,0},{32,16},{48,32},{64,48},{80,64},{96,80},{112,96},{128,112},... | collective-permute-start | bytes 12296 | tf_op jit(solution)/shard_map/ppermute | solution.py:20
  78.8 23.0 %collective-permute-start.2 = (f32[8,1,128]{2,0,1:T(8,128)S(1)}, f32[8,1,128]{2,0,1:T(8,128)S(1)}, u32[]{:S(2)}, u32[]{:S(2)}) collective-permute-start(f32[8,1,128]{2,0,1:T(8,128)S(1)} %copy.120), channel_id=1, source_target_pairs={{0,1},{1,2},{2,3},{3,4},{4,5},{5,6},{6,7},{7,8},{8,9},{9,10},{10,1... | collective-permute-start | bytes 12296 | tf_op jit(solution)/shard_map/ppermute | solution.py:18
  80.8 21.1 %collective-permute-start.3 = (f32[8,1,128]{2,0,1:T(8,128)S(1)}, f32[8,1,128]{2,0,1:T(8,128)S(1)}, u32[]{:S(2)}, u32[]{:S(2)}) collective-permute-start(f32[8,1,128]{2,0,1:T(8,128)S(1)} %copy.121), channel_id=1, source_target_pairs={{1,0},{2,1},{3,2},{4,3},{5,4},{6,5},{7,6},{8,7},{9,8},{10,9},{11,1... | collective-permute-start | bytes 12296 | tf_op jit(solution)/shard_map/ppermute | solution.py:20
  89.3 4.2 copy-start.1
  89.4 8.0 %copy-start.4 = (f32[8192,128]{1,0:T(8,128)S(1)}, f32[8192,128]{1,0:T(8,128)}, u32[]{:S(2)}) copy-start(f32[8192,128]{1,0:T(8,128)} %param.14) | copy-start | bytes 12582916
  93.4 8.0 %copy-start.12 = (s32[4,128]{1,0:T(4,128)S(1)}, s32[4,128]{1,0:T(4,128)}, u32[]{:S(2)}) copy-start(s32[4,128]{1,0:T(4,128)} %param.20) | copy-start | bytes 6148
  324.6 27.4 %collective-permute-start.4 = (f32[8,1,128]{2,0,1:T(8,128)S(1)}, f32[8,1,128]{2,0,1:T(8,128)S(1)}, u32[]{:S(2)}, u32[]{:S(2)}) collective-permute-start(f32[8,1,128]{2,0,1:T(8,128)S(1)} %copy.122), channel_id=1, source_target_pairs={{0,16},{16,32},{32,48},{48,64},{64,80},{80,96},{96,112},{112,128},... | collective-permute-start | bytes 12296 | tf_op jit(solution)/shard_map/ppermute | solution.py:18
  326.2 25.8 %collective-permute-start.5 = (f32[8,1,128]{2,0,1:T(8,128)S(1)}, f32[8,1,128]{2,0,1:T(8,128)S(1)}, u32[]{:S(2)}, u32[]{:S(2)}) collective-permute-start(f32[8,1,128]{2,0,1:T(8,128)S(1)} %copy.123), channel_id=1, source_target_pairs={{16,0},{32,16},{48,32},{64,48},{80,64},{96,80},{112,96},{128,112},... | collective-permute-start | bytes 12296 | tf_op jit(solution)/shard_map/ppermute | solution.py:20
  327.5 24.5 %collective-permute-start.6 = (f32[8,1,128]{2,0,1:T(8,128)S(1)}, f32[8,1,128]{2,0,1:T(8,128)S(1)}, u32[]{:S(2)}, u32[]{:S(2)}) collective-permute-start(f32[8,1,128]{2,0,1:T(8,128)S(1)} %copy.124), channel_id=1, source_target_pairs={{0,1},{1,2},{2,3},{3,4},{4,5},{5,6},{6,7},{7,8},{8,9},{9,10},{10,1... | collective-permute-start | bytes 12296 | tf_op jit(solution)/shard_map/ppermute | solution.py:18
  332.1 19.9 %collective-permute-start.7 = (f32[8,1,128]{2,0,1:T(8,128)S(1)}, f32[8,1,128]{2,0,1:T(8,128)S(1)}, u32[]{:S(2)}, u32[]{:S(2)}) collective-permute-start(f32[8,1,128]{2,0,1:T(8,128)S(1)} %copy.125), channel_id=1, source_target_pairs={{1,0},{2,1},{3,2},{4,3},{5,4},{6,5},{7,6},{8,7},{9,8},{10,9},{11,1... | collective-permute-start | bytes 12296 | tf_op jit(solution)/shard_map/ppermute | solution.py:20
  339.5 4.2 copy-start.2
  339.6 8.0 %copy-start.5 = (f32[8192,128]{1,0:T(8,128)S(1)}, f32[8192,128]{1,0:T(8,128)}, u32[]{:S(2)}) copy-start(f32[8192,128]{1,0:T(8,128)} %param.14) | copy-start | bytes 12582916
  573.4 27.4 %collective-permute-start.10 = (f32[8,1,128]{2,0,1:T(8,128)S(1)}, f32[8,1,128]{2,0,1:T(8,128)S(1)}, u32[]{:S(2)}, u32[]{:S(2)}) collective-permute-start(f32[8,1,128]{2,0,1:T(8,128)S(1)} %copy.128), channel_id=1, source_target_pairs={{0,1},{1,2},{2,3},{3,4},{4,5},{5,6},{6,7},{7,8},{8,9},{9,10},{10,1... | collective-permute-start | bytes 12296 | tf_op jit(solution)/shard_map/ppermute | solution.py:18
  577.3 23.5 %collective-permute-start.11 = (f32[8,1,128]{2,0,1:T(8,128)S(1)}, f32[8,1,128]{2,0,1:T(8,128)S(1)}, u32[]{:S(2)}, u32[]{:S(2)}) collective-permute-start(f32[8,1,128]{2,0,1:T(8,128)S(1)} %copy.129), channel_id=1, source_target_pairs={{1,0},{2,1},{3,2},{4,3},{5,4},{6,5},{7,6},{8,7},{9,8},{10,9},{11,1... | collective-permute-start | bytes 12296 | tf_op jit(solution)/shard_map/ppermute | solution.py:20
  579.2 21.5 %collective-permute-start.8 = (f32[8,1,128]{2,0,1:T(8,128)S(1)}, f32[8,1,128]{2,0,1:T(8,128)S(1)}, u32[]{:S(2)}, u32[]{:S(2)}) collective-permute-start(f32[8,1,128]{2,0,1:T(8,128)S(1)} %copy.126), channel_id=1, source_target_pairs={{0,16},{16,32},{32,48},{48,64},{64,80},{80,96},{96,112},{112,128},... | collective-permute-start | bytes 12296 | tf_op jit(solution)/shard_map/ppermute | solution.py:18
  581.3 19.5 %collective-permute-start.9 = (f32[8,1,128]{2,0,1:T(8,128)S(1)}, f32[8,1,128]{2,0,1:T(8,128)S(1)}, u32[]{:S(2)}, u32[]{:S(2)}) collective-permute-start(f32[8,1,128]{2,0,1:T(8,128)S(1)} %copy.127), channel_id=1, source_target_pairs={{16,0},{32,16},{48,32},{64,48},{80,64},{96,80},{112,96},{128,112},... | collective-permute-start | bytes 12296 | tf_op jit(solution)/shard_map/ppermute | solution.py:20
  588.2 4.2 copy-start.3
  588.4 8.0 %copy-start.6 = (f32[8192,128]{1,0:T(8,128)S(1)}, f32[8192,128]{1,0:T(8,128)}, u32[]{:S(2)}) copy-start(f32[8192,128]{1,0:T(8,128)} %param.14) | copy-start | bytes 12582916
  683.5 64.1 %copy-start.9 = (f32[8,2048]{1,0:T(8,128)}, f32[8,2048]{1,0:T(8,128)S(1)}, u32[]{:S(2)}) copy-start(f32[8,2048]{1,0:T(8,128)S(1)} %get-tuple-element.29) | copy-start | bytes 196612
where the time goes:
time: 753 us; the launch traced here: 748 us
  blocking collectives  633 us (84%)
  matrix products  54.8 us (7%)
  starting transfers between devices  27.5 us (4%)
  other arithmetic  17 us (2%)
  local copies, waits for them, and re-layouts  14.1 us (2%)
    all_gather x4, blocking collectives, precondition(): lax.all_gather(coefficients, ('row', 'col'), axis=1, tiled=True)  252 us
    psum x3, blocking collectives, pair_totals(): lax.psum((jnp.sum(first_field * second_field, axis=1), jnp.sum(third_fiel...  232 us
    psum x2, blocking collectives, shards(): cross_sum = lax.psum(jnp.sum(correction * image, axis=1), ('row', 'col'))  149 us
    dot_general x6, matrix products, sparse_forward(): product = jnp.einsum('lbkw,bkwv->lbv', picked, tile_set, precision=PRECISE)  23.5 us
    dot_general x6, matrix products, sparse_backward(): product = jnp.einsum('lbv,bkwv->lbkw', pieces, tile_set, precision=PRECISE)  21.4 us
    ppermute x6, starting transfers between devices, with_halo(): lax.ppermute(tail, axis, [(i, (i + 1) % count) for i in range(ends)])  16.4 us
  transfers between devices with their start and end apart: 12, of which 0 were waited for; matrix products, arithmetic and copies ran while one was open for 7% of the time, Pallas kernels for 0%

commit v1 on v0

--- a/solution.py
+++ b/solution.py
@@ -5,6 +5,12 @@
 
 ITERS = 3
 PRECISE = lax.Precision.HIGHEST
+
+
+def draw_lines(sheet):
+    for src_i in ("col", "row"):
+        sheet = lax.psum(sheet, axis_name=src_i)
+    return sheet
 
 
 def with_halo(cells, sides, width):
@@ -113,7 +119,7 @@
         residual = residual - step_size * image
         correction = precondition(residual)
         if iteration + 1 < ITERS:
-            cross_sum = lax.psum(jnp.sum(correction * image, axis=1), ("row", "col"))
+            cross_sum = draw_lines(jnp.sum(correction * image, axis=1))
             blend = -cross_sum / curvature_sum
             direction = correction + blend[:, None] * direction
             image = operate(direction)

time: 753 us -> 722 us (0.959)
  blocking collectives: 633 us -> 588 us
  starting transfers between devices: 27.5 us -> 41.7 us
    psum x2 -> x4, blocking collectives: 149 us -> 108 us  [draw_lines(): sheet = lax.psum(sheet, axis_name=src_i)]
    ppermute x6, starting transfers between devices: 16.4 us -> 28.4 us  [with_halo(): lax.ppermute(tail, axis, [(i, (i + 1) % count) for i in range(ends)])]
  transfers between devices with their start and end apart: 12 -> 12, of which waited for: 0 -> 0; matrix products, arithmetic and copies ran while one was open for 7% -> 8% of each run, Pallas kernels for 0% -> 0%
where the time goes in v1:
time: 722 us; the launch traced here: 717 us
  blocking collectives  588 us (81%)
  matrix products  54.8 us (8%)
  starting transfers between devices  41.7 us (6%)
  other arithmetic  16.7 us (2%)
  local copies, waits for them, and re-layouts  14.1 us (2%)
    all_gather x4, blocking collectives, precondition(): lax.all_gather(coefficients, ('row', 'col'), axis=1, tiled=True)  250 us
    psum x3, blocking collectives, pair_totals(): lax.psum((jnp.sum(first_field * second_field, axis=1), jnp.sum(third_fiel...  229 us
    psum x4, blocking collectives, draw_lines(): sheet = lax.psum(sheet, axis_name=src_i)  108 us
    ppermute x6, starting transfers between devices, with_halo(): lax.ppermute(tail, axis, [(i, (i + 1) % count) for i in range(ends)])  28.4 us
    dot_general x6, matrix products, sparse_forward(): product = jnp.einsum('lbkw,bkwv->lbv', picked, tile_set, precision=PRECISE)  23.5 us
    dot_general x6, matrix products, sparse_backward(): product = jnp.einsum('lbv,bkwv->lbkw', pieces, tile_set, precision=PRECISE)  21.4 us
  transfers between devices with their start and end apart: 12, of which 0 were waited for; matrix products, arithmetic and copies ran while one was open for 8% of the time, Pallas kernels for 0%

profile of v1, /device:TPU:1, one launch (start us, length us, event | category | flops | bytes accessed | tf_op | source)
XLA Modules:
  0.0 717.0 jit_solution(17573783131997306341)
XLA Ops:
  0.7 0.8 compare_select_fusion.1
  2.1 1.2 convolution_bitcast_fusion.21
  3.4 67.8 %all-gather = f32[256,32,8]{1,2,0:T(8,128)S(1)} all-gather(f32[1,32,8]{1,2,0:T(8,128)S(1)} %convolution_bitcast_fusion.21), channel_id=1, replica_groups=mesh['row'=16,'col'=16] {'row','col'}, dimensions={0}, use_global_device_ids=true | all-gather | bytes 263168 | tf_op jit(solution)/shard_map/all_gather | solution.py:104
  71.9 0.9 fusion.36
  73.5 1.0 gather_fusion.2
  74.7 2.6 collective-permute-start
  77.4 1.3 collective-permute-start.1
  78.8 1.9 collective-permute-start.2
  80.8 2.6 collective-permute-start.3
  84.7 3.8 convolution_bitcast_fusion.17
  89.3 4.0 convolution_bitcast_fusion.16
  93.3 3.6 convolution_bitcast_fusion.5
  97.3 3.6 convolution_bitcast_fusion.4
  102.1 3.9 scatter_custom_fusion
  106.5 78.0 %all-reduce.2 = (f32[8]{0:T(128)S(1)}, f32[8]{0:T(128)S(1)}) all-reduce(f32[8]{0:T(128)S(1)} %get-tuple-element.10, f32[8]{0:T(128)S(1)} %get-tuple-element.9), channel_id=1, replica_groups=mesh['row'=16,'col'=16] {'row','col'}, use_global_device_ids=true, to_apply=%region_1.2 | all-reduce | flops 16 | bytes 128 | tf_op jit(solution)/shard_map/psum | solution.py:59
  184.8 60.6 %all-gather.1 = f32[256,32,8]{1,2,0:T(8,128)S(1)} all-gather(f32[1,32,8]{1,2,0:T(8,128)S(1)} %convolution_bitcast_fusion.20), channel_id=1, replica_groups=mesh['row'=16,'col'=16] {'row','col'}, dimensions={0}, use_global_device_ids=true | all-gather | bytes 263168 | tf_op jit(solution)/shard_map/all_gather | solution.py:104
  246.1 0.9 fusion.37
  247.4 23.1 %psum.72 = f32[8]{0:T(128)S(1)} all-reduce(f32[8]{0:T(128)S(1)} %get-tuple-element.31), channel_id=1, replica_groups=mesh['row'=16,'col'=16] {'col'}, use_global_device_ids=true, to_apply=%region_6.9 | all-reduce | flops 8 | bytes 64 | tf_op jit(solution)/shard_map/psum | solution.py:12
  270.5 31.0 %psum.73 = f32[8]{0:T(128)S(1)} all-reduce(f32[8]{0:T(128)S(1)} %psum.72), channel_id=1, replica_groups=mesh['row'=16,'col'=16] {'row'}, use_global_device_ids=true, to_apply=%region_7.10 | all-reduce | flops 8 | bytes 64 | tf_op jit(solution)/shard_map/psum | solution.py:12
  301.9 1.0 gather_fusion.5
  303.1 1.3 collective-permute-start.4
  304.5 1.3 collective-permute-start.5
  305.9 10.6 %collective-permute-start.6 = (f32[8,1,128]{2,0,1:T(8,128)S(1)}, f32[8,1,128]{2,0,1:T(8,128)S(1)}, u32[]{:S(2)}, u32[]{:S(2)}) collective-permute-start(f32[8,1,128]{2,0,1:T(8,128)S(1)} %copy.124), channel_id=1, source_target_pairs={{0,1},{1,2},{2,3},{3,4},{4,5},{5,6},{6,7},{7,8},{8,9},{9,10},{10,1... | collective-permute-start | bytes 12296 | tf_op jit(solution)/shard_map/ppermute | solution.py:24
  316.5 3.6 collective-permute-start.7
  320.9 3.8 convolution_bitcast_fusion.15
  325.6 4.0 convolution_bitcast_fusion.14
  329.6 3.6 convolution_bitcast_fusion.3
  333.5 3.6 convolution_bitcast_fusion.2
  338.3 3.9 scatter_custom_fusion.1
  342.6 75.9 %all-reduce.1 = (f32[8]{0:T(128)S(1)}, f32[8]{0:T(128)S(1)}) all-reduce(f32[8]{0:T(128)S(1)} %get-tuple-element.8, f32[8]{0:T(128)S(1)} %get-tuple-element.7), channel_id=1, replica_groups=mesh['row'=16,'col'=16] {'row','col'}, use_global_device_ids=true, to_apply=%region_9.12 | all-reduce | flops 16 | bytes 128 | tf_op jit(solution)/shard_map/psum | solution.py:59
  418.9 60.8 %all-gather.2 = f32[256,32,8]{1,2,0:T(8,128)S(1)} all-gather(f32[1,32,8]{1,2,0:T(8,128)S(1)} %convolution_bitcast_fusion.19), channel_id=1, replica_groups=mesh['row'=16,'col'=16] {'row','col'}, dimensions={0}, use_global_device_ids=true | all-gather | bytes 263168 | tf_op jit(solution)/shard_map/all_gather | solution.py:104
  480.4 0.9 fusion.38
  481.7 23.1 %psum.76 = f32[8]{0:T(128)S(1)} all-reduce(f32[8]{0:T(128)S(1)} %get-tuple-element.33), channel_id=1, replica_groups=mesh['row'=16,'col'=16] {'col'}, use_global_device_ids=true, to_apply=%region_14.17 | all-reduce | flops 8 | bytes 64 | tf_op jit(solution)/shard_map/psum | solution.py:12
  504.8 30.9 %psum.77 = f32[8]{0:T(128)S(1)} all-reduce(f32[8]{0:T(128)S(1)} %psum.76), channel_id=1, replica_groups=mesh['row'=16,'col'=16] {'row'}, use_global_device_ids=true, to_apply=%region_15.18 | all-reduce | flops 8 | bytes 64 | tf_op jit(solution)/shard_map/psum | solution.py:12
  536.1 1.0 gather_fusion.8
  537.3 10.6 %collective-permute-start.10 = (f32[8,1,128]{2,0,1:T(8,128)S(1)}, f32[8,1,128]{2,0,1:T(8,128)S(1)}, u32[]{:S(2)}, u32[]{:S(2)}) collective-permute-start(f32[8,1,128]{2,0,1:T(8,128)S(1)} %copy.128), channel_id=1, source_target_pairs={{0,1},{1,2},{2,3},{3,4},{4,5},{5,6},{6,7},{7,8},{8,9},{9,10},{10,1... | collective-permute-start | bytes 12296 | tf_op jit(solution)/shard_map/ppermute | solution.py:24
  548.0 3.1 collective-permute-start.11
  551.2 1.3 collective-permute-start.8
  552.6 1.3 collective-permute-start.9
  554.7 3.8 convolution_bitcast_fusion.13
  559.3 4.0 convolution_bitcast_fusion.12
  563.3 3.6 convolution_bitcast_fusion.1
  567.3 3.6 convolution_bitcast_fusion
  572.1 3.9 scatter_custom_fusion.2
  576.5 75.5 %all-reduce = (f32[8]{0:T(128)S(1)}, f32[8]{0:T(128)S(1)}) all-reduce(f32[8]{0:T(128)S(1)} %get-tuple-element.6, f32[8]{0:T(128)S(1)} %get-tuple-element.5), channel_id=1, replica_groups=mesh['row'=16,'col'=16] {'row','col'}, use_global_device_ids=true, to_apply=%region_17.20 | all-reduce | flops 16 | bytes 128 | tf_op jit(solution)/shard_map/psum | solution.py:59
  653.0 61.2 %all-gather.3 = f32[256,32,8]{1,2,0:T(8,128)S(1)} all-gather(f32[1,32,8]{1,2,0:T(8,128)S(1)} %convolution_bitcast_fusion.18), channel_id=1, replica_groups=mesh['row'=16,'col'=16] {'row','col'}, dimensions={0}, use_global_device_ids=true | all-gather | bytes 263168 | tf_op jit(solution)/shard_map/all_gather | solution.py:104
  714.9 0.9 fusion.39
  715.8 0.9 convolution_add_fusion
  (139 shorter events, 19.4 us)
Async XLA Ops:
  0.6 71.3 %copy-start = (f32[32,8192]{1,0:T(8,128)S(1)}, f32[32,8192]{1,0:T(8,128)}, u32[]{:S(2)}) copy-start(f32[32,8192]{1,0:T(8,128)} %param.19) | copy-start | bytes 3145732
  0.6 72.2 %copy-start.8 = (f32[8,2048]{1,0:T(8,128)S(1)}, f32[8,2048]{1,0:T(8,128)}, u32[]{:S(2)}) copy-start(f32[8,2048]{1,0:T(8,128)} %param.13) | copy-start | bytes 196612
  0.7 72.2 %copy-start.7 = (f32[32,2048]{1,0:T(8,128)S(1)}, f32[32,2048]{1,0:T(8,128)}, u32[]{:S(2)}) copy-start(f32[32,2048]{1,0:T(8,128)} %param.18) | copy-start | bytes 786436
  3.4 80.0 %copy-start.11 = (s32[16,4]{0,1:T(4,128)S(1)}, s32[16,4]{0,1:T(4,128)}, u32[]{:S(2)}) copy-start(s32[16,4]{0,1:T(4,128)} %param.15) | copy-start | bytes 772
  3.4 80.2 %copy-start.10 = (s32[16,4]{0,1:T(4,128)S(1)}, s32[16,4]{0,1:T(4,128)}, u32[]{:S(2)}) copy-start(s32[16,4]{0,1:T(4,128)} %param.17) | copy-start | bytes 772
  3.4 80.4 %copy-start.13 = (s32[1,4]{1,0:T(1,128)S(1)}, s32[1,4]{1,0:T(1,128)}, u32[]{:S(2)}) copy-start(s32[1,4]{1,0:T(1,128)} %param.21) | copy-start | bytes 52
  74.7 27.0 %collective-permute-start = (f32[8,1,128]{2,0,1:T(8,128)S(1)}, f32[8,1,128]{2,0,1:T(8,128)S(1)}, u32[]{:S(2)}, u32[]{:S(2)}) collective-permute-start(f32[8,1,128]{2,0,1:T(8,128)S(1)} %copy.118), channel_id=1, source_target_pairs={{0,16},{16,32},{32,48},{48,64},{64,80},{80,96},{96,112},{112,128},... | collective-permute-start | bytes 12296 | tf_op jit(solution)/shard_map/ppermute | solution.py:24
  77.4 24.3 %collective-permute-start.1 = (f32[8,1,128]{2,0,1:T(8,128)S(1)}, f32[8,1,128]{2,0,1:T(8,128)S(1)}, u32[]{:S(2)}, u32[]{:S(2)}) collective-permute-start(f32[8,1,128]{2,0,1:T(8,128)S(1)} %copy.119), channel_id=1, source_target_pairs={{16,0},{32,16},{48,32},{64,48},{80,64},{96,80},{112,96},{128,112},... | collective-permute-start | bytes 12296 | tf_op jit(solution)/shard_map/ppermute | solution.py:26
  78.8 22.9 %collective-permute-start.2 = (f32[8,1,128]{2,0,1:T(8,128)S(1)}, f32[8,1,128]{2,0,1:T(8,128)S(1)}, u32[]{:S(2)}, u32[]{:S(2)}) collective-permute-start(f32[8,1,128]{2,0,1:T(8,128)S(1)} %copy.120), channel_id=1, source_target_pairs={{0,1},{1,2},{2,3},{3,4},{4,5},{5,6},{6,7},{7,8},{8,9},{9,10},{10,1... | collective-permute-start | bytes 12296 | tf_op jit(solution)/shard_map/ppermute | solution.py:24
  80.8 20.9 %collective-permute-start.3 = (f32[8,1,128]{2,0,1:T(8,128)S(1)}, f32[8,1,128]{2,0,1:T(8,128)S(1)}, u32[]{:S(2)}, u32[]{:S(2)}) collective-permute-start(f32[8,1,128]{2,0,1:T(8,128)S(1)} %copy.121), channel_id=1, source_target_pairs={{1,0},{2,1},{3,2},{4,3},{5,4},{6,5},{7,6},{8,7},{9,8},{10,9},{11,1... | collective-permute-start | bytes 12296 | tf_op jit(solution)/shard_map/ppermute | solution.py:26
  89.2 4.2 copy-start.1
  89.3 8.0 %copy-start.4 = (f32[8192,128]{1,0:T(8,128)S(1)}, f32[8192,128]{1,0:T(8,128)}, u32[]{:S(2)}) copy-start(f32[8192,128]{1,0:T(8,128)} %param.14) | copy-start | bytes 12582916
  93.3 8.0 %copy-start.12 = (s32[4,128]{1,0:T(4,128)S(1)}, s32[4,128]{1,0:T(4,128)}, u32[]{:S(2)}) copy-start(s32[4,128]{1,0:T(4,128)} %param.20) | copy-start | bytes 6148
  303.1 34.8 %collective-permute-start.4 = (f32[8,1,128]{2,0,1:T(8,128)S(1)}, f32[8,1,128]{2,0,1:T(8,128)S(1)}, u32[]{:S(2)}, u32[]{:S(2)}) collective-permute-start(f32[8,1,128]{2,0,1:T(8,128)S(1)} %copy.122), channel_id=1, source_target_pairs={{0,16},{16,32},{32,48},{48,64},{64,80},{80,96},{96,112},{112,128},... | collective-permute-start | bytes 12296 | tf_op jit(solution)/shard_map/ppermute | solution.py:24
  304.5 33.4 %collective-permute-start.5 = (f32[8,1,128]{2,0,1:T(8,128)S(1)}, f32[8,1,128]{2,0,1:T(8,128)S(1)}, u32[]{:S(2)}, u32[]{:S(2)}) collective-permute-start(f32[8,1,128]{2,0,1:T(8,128)S(1)} %copy.123), channel_id=1, source_target_pairs={{16,0},{32,16},{48,32},{64,48},{80,64},{96,80},{112,96},{128,112},... | collective-permute-start | bytes 12296 | tf_op jit(solution)/shard_map/ppermute | solution.py:26
  305.9 32.1 %collective-permute-start.6 = (f32[8,1,128]{2,0,1:T(8,128)S(1)}, f32[8,1,128]{2,0,1:T(8,128)S(1)}, u32[]{:S(2)}, u32[]{:S(2)}) collective-permute-start(f32[8,1,128]{2,0,1:T(8,128)S(1)} %copy.124), channel_id=1, source_target_pairs={{0,1},{1,2},{2,3},{3,4},{4,5},{5,6},{6,7},{7,8},{8,9},{9,10},{10,1... | collective-permute-start | bytes 12296 | tf_op jit(solution)/shard_map/ppermute | solution.py:24
  316.5 21.4 %collective-permute-start.7 = (f32[8,1,128]{2,0,1:T(8,128)S(1)}, f32[8,1,128]{2,0,1:T(8,128)S(1)}, u32[]{:S(2)}, u32[]{:S(2)}) collective-permute-start(f32[8,1,128]{2,0,1:T(8,128)S(1)} %copy.125), channel_id=1, source_target_pairs={{1,0},{2,1},{3,2},{4,3},{5,4},{6,5},{7,6},{8,7},{9,8},{10,9},{11,1... | collective-permute-start | bytes 12296 | tf_op jit(solution)/shard_map/ppermute | solution.py:26
  325.4 4.2 copy-start.2
  325.6 8.0 %copy-start.5 = (f32[8192,128]{1,0:T(8,128)S(1)}, f32[8192,128]{1,0:T(8,128)}, u32[]{:S(2)}) copy-start(f32[8192,128]{1,0:T(8,128)} %param.14) | copy-start | bytes 12582916
  537.3 34.3 %collective-permute-start.10 = (f32[8,1,128]{2,0,1:T(8,128)S(1)}, f32[8,1,128]{2,0,1:T(8,128)S(1)}, u32[]{:S(2)}, u32[]{:S(2)}) collective-permute-start(f32[8,1,128]{2,0,1:T(8,128)S(1)} %copy.128), channel_id=1, source_target_pairs={{0,1},{1,2},{2,3},{3,4},{4,5},{5,6},{6,7},{7,8},{8,9},{9,10},{10,1... | collective-permute-start | bytes 12296 | tf_op jit(solution)/shard_map/ppermute | solution.py:24
  548.0 23.6 %collective-permute-start.11 = (f32[8,1,128]{2,0,1:T(8,128)S(1)}, f32[8,1,128]{2,0,1:T(8,128)S(1)}, u32[]{:S(2)}, u32[]{:S(2)}) collective-permute-start(f32[8,1,128]{2,0,1:T(8,128)S(1)} %copy.129), channel_id=1, source_target_pairs={{1,0},{2,1},{3,2},{4,3},{5,4},{6,5},{7,6},{8,7},{9,8},{10,9},{11,1... | collective-permute-start | bytes 12296 | tf_op jit(solution)/shard_map/ppermute | solution.py:26
  551.2 20.4 %collective-permute-start.8 = (f32[8,1,128]{2,0,1:T(8,128)S(1)}, f32[8,1,128]{2,0,1:T(8,128)S(1)}, u32[]{:S(2)}, u32[]{:S(2)}) collective-permute-start(f32[8,1,128]{2,0,1:T(8,128)S(1)} %copy.126), channel_id=1, source_target_pairs={{0,16},{16,32},{32,48},{48,64},{64,80},{80,96},{96,112},{112,128},... | collective-permute-start | bytes 12296 | tf_op jit(solution)/shard_map/ppermute | solution.py:24
  552.6 19.1 %collective-permute-start.9 = (f32[8,1,128]{2,0,1:T(8,128)S(1)}, f32[8,1,128]{2,0,1:T(8,128)S(1)}, u32[]{:S(2)}, u32[]{:S(2)}) collective-permute-start(f32[8,1,128]{2,0,1:T(8,128)S(1)} %copy.127), channel_id=1, source_target_pairs={{16,0},{32,16},{48,32},{64,48},{80,64},{96,80},{112,96},{128,112},... | collective-permute-start | bytes 12296 | tf_op jit(solution)/shard_map/ppermute | solution.py:26
  559.2 4.2 copy-start.3
  559.3 8.0 %copy-start.6 = (f32[8192,128]{1,0:T(8,128)S(1)}, f32[8192,128]{1,0:T(8,128)}, u32[]{:S(2)}) copy-start(f32[8192,128]{1,0:T(8,128)} %param.14) | copy-start | bytes 12582916
  652.7 64.0 %copy-start.9 = (f32[8,2048]{1,0:T(8,128)}, f32[8,2048]{1,0:T(8,128)S(1)}, u32[]{:S(2)}) copy-start(f32[8,2048]{1,0:T(8,128)S(1)} %get-tuple-element.29) | copy-start | bytes 196612
